TPU v7x, 128 devices: a whole 4x4x4 slice. The times are simulated.
128 devices in a mesh: row: 8 (over y_hi, x), col: 16 (over y_lo, z, core).
Axes of the slice: x: 4, y: 4 (y_hi: 2, y_lo: 2; y = y_hi * 2 + y_lo), z: 4, core: 2. Of those that a mesh axis runs over, the one named last changes fastest.
Arguments:
- front_orig: float32 [12288, 12288], P('row', 'col')
- pivot_shift: float32 [12288], replicated, may hold values from 4.5 to 9
- child_update: float32 [16384, 8192], P('row', 'col'), may hold values from -0.046875 to 0.046875
- child_map: int32 [2, 32], replicated, may hold values from 0 to 47, as said below
Outputs:
- front_out: float32 [12288, 12288], P('row', 'col')
Inputs may be any that keep to these rules, and one draw needn't show every extreme that they name: Child h's block b (rows and columns alike) goes to parent block child_map[h, b]; child_map[h, b] % 16 == b % 16; the two child blocks b and b + 16 (b < 16) take two different ones of the parent blocks b, b + 16, b + 32, the smaller child block to the smaller parent block.
All inputs are finite; a program needn't handle non-finite values.
Results may differ from a plain program's by a relative error of at most 0.0001.
Values sent between devices are 32-bit elements; how exact they have to be, the bound alone decides.
No kernel may reach another device: no remote copies, remote signals or barrier semaphores. Data moves between devices by JAX's collectives and lax.ppermute only.
A program may use at most 128 MiB of HBM per device.

v0:
```python
import jax
import jax.numpy as jnp
from jax import lax
from jax.sharding import PartitionSpec as P

BS = 256
PANELS = 6


def from_partner(shard, axis, apart):
    return lax.ppermute(shard, axis, [(i, i ^ 1 << apart) for i in range(lax.axis_size(axis))])


def from_root(shard, axis, root):
    mine = lax.axis_index(axis) == root
    return lax.psum(jnp.where(mine, shard, jnp.zeros_like(shard)), axis)


def symmetric_block(pivot_block):
    return jnp.tril(pivot_block) + jnp.tril(pivot_block, -1).T


def factor_rows(pivot, panel_rows):
    factor = jnp.linalg.cholesky(symmetric_block(pivot))
    below = lax.linalg.triangular_solve(
        factor, panel_rows, left_side=False, lower=True, transpose_a=True
    )
    return (factor, below)


def on_device(front_orig, pivot_shift, child_update, child_map):
    n_row = lax.axis_size("row")
    n_col = lax.axis_size("col")
    row_id = lax.axis_index("row")
    col_id = lax.axis_index("col")
    half_rows = n_row // 2
    local_rows = front_orig.shape[0] // BS
    local_cols = front_orig.shape[1] // BS
    child_rows = child_update.shape[0] // BS
    child_cols = child_update.shape[1] // BS
    pair_count = child_rows // 2
    child_side = row_id // half_rows
    inner_row = row_id % half_rows
    holds_first = child_side == 0
    paired = child_update.reshape(pair_count, 2, BS, child_cols * BS)
    even_blocks = paired[:, 0]
    odd_blocks = paired[:, 1]
    outgoing = jnp.where(holds_first, odd_blocks, even_blocks)
    staying = jnp.where(holds_first, even_blocks, odd_blocks)
    arrived = from_partner(outgoing, "row", half_rows.bit_length() - 1)
    first_part = jnp.where(holds_first, staying, arrived)
    second_part = jnp.where(holds_first, arrived, staying)
    table_index = jnp.arange(child_map.shape[1], dtype=jnp.int32)
    row_wanted = (2 * jnp.arange(pair_count, dtype=jnp.int32) + child_side) * half_rows + inner_row
    col_wanted = jnp.arange(child_cols, dtype=jnp.int32) * n_col + col_id

    def lookup(targets, wanted):
        return jnp.sum(
            jnp.where(wanted[:, None] == table_index[None, :], targets[None, :], 0), axis=1
        )

    def place(part, child_id):
        targets = child_map[child_id]
        row_target = lookup(targets, row_wanted) // n_row
        col_target = lookup(targets, col_wanted) // n_col
        row_pick = (row_target[None, :] == jnp.arange(local_rows, dtype=jnp.int32)[:, None]).astype(
            jnp.float32
        )
        col_pick = (col_target[None, :] == jnp.arange(local_cols, dtype=jnp.int32)[:, None]).astype(
            jnp.float32
        )
        tiles = part.reshape(pair_count, BS, child_cols, BS)
        placed = jnp.einsum(
            "pq,qsjt,kj->pskt", row_pick, tiles, col_pick, precision=lax.Precision.HIGHEST
        )
        return placed.reshape(local_rows * BS, local_cols * BS)

    row_blocks = jnp.arange(local_rows, dtype=jnp.int32) * n_row + row_id
    col_blocks = jnp.arange(local_cols, dtype=jnp.int32) * n_col + col_id
    offsets = jnp.arange(BS, dtype=jnp.int32)
    row_index = (row_blocks[:, None] * BS + offsets[None, :]).reshape(-1)
    col_index = (col_blocks[:, None] * BS + offsets[None, :]).reshape(-1)
    shift_rows = lax.dynamic_index_in_dim(
        pivot_shift.reshape(local_rows, n_row, BS), row_id, axis=1, keepdims=False
    ).reshape(-1)
    diag_term = jnp.where(row_index[:, None] == col_index[None, :], shift_rows[:, None], 0.0)
    front_now = front_orig + diag_term
    front_now = front_now + place(first_part, 0)
    front_now = front_now + place(second_part, 1)
    row_of = jnp.repeat(row_blocks, BS)
    col_of = jnp.repeat(col_blocks, BS)
    stride = n_col // n_row
    pick_index = jnp.arange(local_cols, dtype=jnp.int32) * stride + col_id // n_row
    pick_table = (pick_index[:, None] == jnp.arange(local_rows, dtype=jnp.int32)[None, :]).astype(
        jnp.float32
    )
    level = row_blocks[:, None, None]
    for panel_id in range(PANELS):
        owner_row = panel_id % n_row
        owner_col = panel_id % n_col
        row_slot = panel_id // n_row
        col_slot = panel_id // n_col
        column = front_now[:, col_slot * BS : (col_slot + 1) * BS]
        pivot_local = column[row_slot * BS : (row_slot + 1) * BS]
        pivot = from_root(pivot_local, "row", owner_row)
        factor, own_rows = factor_rows(pivot, column)
        below = from_root(own_rows, "col", owner_col)
        chosen = jnp.einsum(
            "jp,pst->jst",
            pick_table,
            below.reshape(local_rows, BS, BS),
            precision=lax.Precision.HIGHEST,
        )
        across = from_root(chosen.reshape(local_cols * BS, BS), "row", col_id % n_row)
        live = (row_of > panel_id)[:, None] & (col_of > panel_id)[None, :]
        update = jnp.einsum("rk,ck->rc", below, across, precision=lax.Precision.HIGHEST)
        front_now = front_now - jnp.where(live, update, 0.0)
        tiles_now = column.reshape(local_rows, BS, BS)
        below_tiles = below.reshape(local_rows, BS, BS)
        new_column = jnp.where(
            level > panel_id, below_tiles, jnp.where(level == panel_id, factor[None], tiles_now)
        )
        new_column = new_column.reshape(local_rows * BS, BS)
        kept_column = front_now[:, col_slot * BS : (col_slot + 1) * BS]
        front_now = front_now.at[:, col_slot * BS : (col_slot + 1) * BS].set(
            jnp.where(col_id == owner_col, new_column, kept_column)
        )
    return front_now


def solution(mesh):
    in_specs = (P("row", "col"), P(), P("row", "col"), P())
    out_specs = P("row", "col")
    return jax.shard_map(
        on_device, mesh=mesh, in_specs=in_specs, out_specs=out_specs, check_vma=False
    )
```

profile of v0, /device:TPU:0, one launch (start us, length us, event | category | flops | bytes accessed | tf_op | source)
XLA Modules:
  0.0 2403.0 jit_solution(18215019468247353154)
XLA Ops:
  19.4 39.0 %collective-permute-done = f32[4,256,512]{2,1,0:T(8,128)} collective-permute-done((f32[4,256,512]{2,1,0:T(8,128)S(1)}, f32[4,256,512]{2,1,0:T(8,128)}, u32[]{:S(2)}, u32[]{:S(2)}) %collective-permute-start) | collective-permute-done | bytes 2097184 | tf_op jit(solution)/shard_map/ppermute | solution.py:11
  126.6 86.2 %all-reduce.20.cloned.1.call-done = f32[256,256]{0,1:T(8,128)} async-done(((f32[256,256]{0,1:T(8,128)}), f32[256,256]{0,1:T(8,128)}) %all-reduce.20.cloned.1.call-update) | async-done | bytes 262160 | tf_op jit(solution)/shard_map/psum | solution.py:16
  256.5 19.7 custom-call.22
  282.3 119.5 %all-reduce.22.cloned.1.call-done = f32[1536,256]{0,1:T(8,128)} async-done(((f32[1536,256]{0,1:T(8,128)}), f32[1536,256]{0,1:T(8,128)}) %all-reduce.22.cloned.1.call-update) | async-done | bytes 1572880 | tf_op jit(solution)/shard_map/psum | solution.py:16
  409.5 84.5 %all-reduce.24.cloned.1.call-done = f32[768,256]{1,0:T(8,128)} async-done(((f32[768,256]{1,0:T(8,128)}), f32[768,256]{1,0:T(8,128)}) %all-reduce.24.cloned.1.call-update) | async-done | bytes 786448 | tf_op jit(solution)/shard_map/psum | solution.py:16
  507.4 82.4 %all-reduce.26.cloned.1.call-done = f32[256,256]{0,1:T(8,128)} async-done(((f32[256,256]{0,1:T(8,128)}), f32[256,256]{0,1:T(8,128)}) %all-reduce.26.cloned.1.call-update) | async-done | bytes 262160 | tf_op jit(solution)/shard_map/psum | solution.py:16
  632.5 19.7 custom-call.24
  656.0 119.5 %all-reduce.28.cloned.1.call-done = f32[1536,256]{0,1:T(8,128)} async-done(((f32[1536,256]{0,1:T(8,128)}), f32[1536,256]{0,1:T(8,128)}) %all-reduce.28.cloned.1.call-update) | async-done | bytes 1572880 | tf_op jit(solution)/shard_map/psum | solution.py:16
  785.3 82.6 %all-reduce.30.cloned.1.call-done = f32[768,256]{1,0:T(8,128)} async-done(((f32[768,256]{1,0:T(8,128)}), f32[768,256]{1,0:T(8,128)}) %all-reduce.30.cloned.1.call-update) | async-done | bytes 786448 | tf_op jit(solution)/shard_map/psum | solution.py:16
  883.5 82.2 %all-reduce.32.cloned.1.call-done = f32[256,256]{1,0:T(8,128)} async-done(((f32[256,256]{1,0:T(8,128)}), f32[256,256]{1,0:T(8,128)}) %all-reduce.32.cloned.1.call-update) | async-done | bytes 262160 | tf_op jit(solution)/shard_map/psum | solution.py:16
  1008.7 19.7 custom-call.26
  1032.9 119.5 %all-reduce.34.cloned.1.call-done = f32[1536,256]{0,1:T(8,128)} async-done(((f32[1536,256]{0,1:T(8,128)}), f32[1536,256]{0,1:T(8,128)}) %all-reduce.34.cloned.1.call-update) | async-done | bytes 1572880 | tf_op jit(solution)/shard_map/psum | solution.py:16
  1168.1 76.5 %all-reduce.36.cloned.1.call-done = f32[768,256]{1,0:T(8,128)} async-done(((f32[768,256]{1,0:T(8,128)}), f32[768,256]{1,0:T(8,128)}) %all-reduce.36.cloned.1.call-update) | async-done | bytes 786448 | tf_op jit(solution)/shard_map/psum | solution.py:16
  1263.0 82.1 %all-reduce.38.cloned.1.call-done = f32[256,256]{1,0:T(8,128)} async-done(((f32[256,256]{1,0:T(8,128)}), f32[256,256]{1,0:T(8,128)}) %all-reduce.38.cloned.1.call-update) | async-done | bytes 262160 | tf_op jit(solution)/shard_map/psum | solution.py:16
  1388.1 19.7 custom-call.28
  1412.3 119.5 %all-reduce.40.cloned.1.call-done = f32[1536,256]{0,1:T(8,128)} async-done(((f32[1536,256]{0,1:T(8,128)}), f32[1536,256]{0,1:T(8,128)}) %all-reduce.40.cloned.1.call-update) | async-done | bytes 1572880 | tf_op jit(solution)/shard_map/psum | solution.py:16
  1537.1 87.0 %all-reduce.42.cloned.1.call-done = f32[768,256]{1,0:T(8,128)} async-done(((f32[768,256]{1,0:T(8,128)}), f32[768,256]{1,0:T(8,128)}) %all-reduce.42.cloned.1.call-update) | async-done | bytes 786448 | tf_op jit(solution)/shard_map/psum | solution.py:16
  1642.1 82.2 %all-reduce.44.cloned.1.call-done = f32[256,256]{1,0:T(8,128)} async-done(((f32[256,256]{1,0:T(8,128)}), f32[256,256]{1,0:T(8,128)}) %all-reduce.44.cloned.1.call-update) | async-done | bytes 262160 | tf_op jit(solution)/shard_map/psum | solution.py:16
  1791.4 119.5 %all-reduce.46.cloned.1.call-done = f32[1536,256]{0,1:T(8,128)} async-done(((f32[1536,256]{0,1:T(8,128)}), f32[1536,256]{0,1:T(8,128)}) %all-reduce.46.cloned.1.call-update) | async-done | bytes 1572880 | tf_op jit(solution)/shard_map/psum | solution.py:16
  1916.2 87.0 %all-reduce.48.cloned.1.call-done = f32[768,256]{1,0:T(8,128)} async-done(((f32[768,256]{1,0:T(8,128)}), f32[768,256]{1,0:T(8,128)}) %all-reduce.48.cloned.1.call-update) | async-done | bytes 786448 | tf_op jit(solution)/shard_map/psum | solution.py:16
  2017.6 82.1 %all-reduce.50.cloned.1.call-done = f32[256,256]{1,0:T(8,128)} async-done(((f32[256,256]{1,0:T(8,128)}), f32[256,256]{1,0:T(8,128)}) %all-reduce.50.cloned.1.call-update) | async-done | bytes 262160 | tf_op jit(solution)/shard_map/psum | solution.py:16
  2142.9 19.7 custom-call.32
  2167.1 119.5 %all-reduce.52.cloned.1.call-done = f32[1536,256]{0,1:T(8,128)} async-done(((f32[1536,256]{0,1:T(8,128)}), f32[1536,256]{0,1:T(8,128)}) %all-reduce.52.cloned.1.call-update) | async-done | bytes 1572880 | tf_op jit(solution)/shard_map/psum | solution.py:16
  2293.8 85.0 %all-reduce.54.cloned.1.call-done = f32[768,256]{1,0:T(8,128)} async-done(((f32[768,256]{1,0:T(8,128)}), f32[768,256]{1,0:T(8,128)}) %all-reduce.54.cloned.1.call-update) | async-done | bytes 786448 | tf_op jit(solution)/shard_map/psum | solution.py:16
  (390 shorter events, 549.7 us)
Async XLA Ops:
  6.5 206.3 %all-reduce.20.cloned.1.call-start = ((), (), s32[]{:S(2)}) async-start(), calls=%async_computation | async-start | bytes 524288 | tf_op jit(solution)/shard_map/psum | solution.py:16
  9.2 49.1 %collective-permute-start = (f32[4,256,512]{2,1,0:T(8,128)S(1)}, f32[4,256,512]{2,1,0:T(8,128)}, u32[]{:S(2)}, u32[]{:S(2)}) collective-permute-start(f32[4,256,512]{2,1,0:T(8,128)S(1)} %select_bitcast_fusion), channel_id=1, source_target_pairs={{0,64},{16,80},{32,96},{48,112},{64,0},{80,16},{96,32},{112,48},{1... | collective-permute-start | bytes 6291464 | tf_op jit(solution)/shard_map/ppermute | solution.py:11
  125.9 275.9 %all-reduce.22.cloned.1.call-start = ((), (), s32[]{:S(2)}) async-start(), calls=%async_computation.1 | async-start | bytes 3145728 | tf_op jit(solution)/shard_map/psum | solution.py:16
  282.2 211.8 %all-reduce.24.cloned.1.call-start = ((), (), s32[]{:S(2)}) async-start(), calls=%async_computation.2 | async-start | bytes 1572864 | tf_op jit(solution)/shard_map/psum | solution.py:16
  406.7 183.1 %all-reduce.26.cloned.1.call-start = ((), (), s32[]{:S(2)}) async-start(), calls=%async_computation.3 | async-start | bytes 524288 | tf_op jit(solution)/shard_map/psum | solution.py:16
  407.9 86.2 %copy-start.9 = (f32[1536,256]{0,1:T(8,128)S(1)}, f32[1536,256]{0,1:T(8,128)}, u32[]{:S(2)}) copy-start(f32[1536,256]{0,1:T(8,128)} %all-reduce.22.cloned.1.call-done) | copy-start | bytes 4718596
  507.1 268.4 %all-reduce.28.cloned.1.call-start = ((), (), s32[]{:S(2)}) async-start(), calls=%async_computation.4 | async-start | bytes 3145728 | tf_op jit(solution)/shard_map/psum | solution.py:16
  656.0 211.9 %all-reduce.30.cloned.1.call-start = ((), (), s32[]{:S(2)}) async-start(), calls=%async_computation.5 | async-start | bytes 1572864 | tf_op jit(solution)/shard_map/psum | solution.py:16
  780.5 185.1 %all-reduce.32.cloned.1.call-start = ((), (), s32[]{:S(2)}) async-start(), calls=%async_computation.6 | async-start | bytes 524288 | tf_op jit(solution)/shard_map/psum | solution.py:16
  782.2 85.8 %copy-start.10 = (f32[1536,256]{0,1:T(8,128)S(1)}, f32[1536,256]{0,1:T(8,128)}, u32[]{:S(2)}) copy-start(f32[1536,256]{0,1:T(8,128)} %all-reduce.28.cloned.1.call-done) | copy-start | bytes 4718596
  883.0 269.4 %all-reduce.34.cloned.1.call-start = ((), (), s32[]{:S(2)}) async-start(), calls=%async_computation.7 | async-start | bytes 3145728 | tf_op jit(solution)/shard_map/psum | solution.py:16
  1032.8 211.8 %all-reduce.36.cloned.1.call-start = ((), (), s32[]{:S(2)}) async-start(), calls=%async_computation.8 | async-start | bytes 1572864 | tf_op jit(solution)/shard_map/psum | solution.py:16
  1157.3 187.9 %all-reduce.38.cloned.1.call-start = ((), (), s32[]{:S(2)}) async-start(), calls=%async_computation.9 | async-start | bytes 524288 | tf_op jit(solution)/shard_map/psum | solution.py:16
  1262.6 269.3 %all-reduce.40.cloned.1.call-start = ((), (), s32[]{:S(2)}) async-start(), calls=%async_computation.10 | async-start | bytes 3145728 | tf_op jit(solution)/shard_map/psum | solution.py:16
  1412.3 211.9 %all-reduce.42.cloned.1.call-start = ((), (), s32[]{:S(2)}) async-start(), calls=%async_computation.11 | async-start | bytes 1572864 | tf_op jit(solution)/shard_map/psum | solution.py:16
  1535.7 88.4 %copy-start.12 = (f32[1536,256]{0,1:T(8,128)S(1)}, f32[1536,256]{0,1:T(8,128)}, u32[]{:S(2)}) copy-start(f32[1536,256]{0,1:T(8,128)} %all-reduce.40.cloned.1.call-done) | copy-start | bytes 4718596
  1536.7 187.5 %all-reduce.44.cloned.1.call-start = ((), (), s32[]{:S(2)}) async-start(), calls=%async_computation.12 | async-start | bytes 524288 | tf_op jit(solution)/shard_map/psum | solution.py:16
  1640.9 146.9 %copy-start.4 = (f32[1536,256]{1,0:T(8,128)}, f32[1536,256]{1,0:T(8,128)S(1)}, u32[]{:S(2)}) copy-start(f32[1536,256]{1,0:T(8,128)S(1)} %get-tuple-element.244) | copy-start | bytes 4718596
  1641.6 269.3 %all-reduce.46.cloned.1.call-start = ((), (), s32[]{:S(2)}) async-start(), calls=%async_computation.13 | async-start | bytes 3145728 | tf_op jit(solution)/shard_map/psum | solution.py:16
  1791.4 211.8 %all-reduce.48.cloned.1.call-start = ((), (), s32[]{:S(2)}) async-start(), calls=%async_computation.14 | async-start | bytes 1572864 | tf_op jit(solution)/shard_map/psum | solution.py:16
  1914.8 88.4 %copy-start.13 = (f32[1536,256]{0,1:T(8,128)S(1)}, f32[1536,256]{0,1:T(8,128)}, u32[]{:S(2)}) copy-start(f32[1536,256]{0,1:T(8,128)} %all-reduce.46.cloned.1.call-done) | copy-start | bytes 4718596
  1915.8 183.9 %all-reduce.50.cloned.1.call-start = ((), (), s32[]{:S(2)}) async-start(), calls=%async_computation.15 | async-start | bytes 524288 | tf_op jit(solution)/shard_map/psum | solution.py:16
  2017.2 269.4 %all-reduce.52.cloned.1.call-start = ((), (), s32[]{:S(2)}) async-start(), calls=%async_computation.16 | async-start | bytes 3145728 | tf_op jit(solution)/shard_map/psum | solution.py:16
  2167.0 211.8 %all-reduce.54.cloned.1.call-start = ((), (), s32[]{:S(2)}) async-start(), calls=%async_computation.17 | async-start | bytes 1572864 | tf_op jit(solution)/shard_map/psum | solution.py:16
  (17 other events, 155.1 us)
Sparse Core Ops, SparseCore 0:
  126.0 86.8 all-reduce.19
  282.4 119.3 all-reduce.21
  406.8 87.1 all-reduce.23
  507.3 82.4 all-reduce.25
  656.1 119.3 all-reduce.27
  780.7 87.2 all-reduce.29
  883.1 82.4 all-reduce.31
  1032.9 119.3 all-reduce.33
  1157.4 87.1 all-reduce.35
  1262.7 82.4 all-reduce.37
  1412.4 119.4 all-reduce.39
  1536.9 87.2 all-reduce.41
  1641.8 82.4 all-reduce.43
  1791.5 119.3 all-reduce.45
  1916.0 87.1 all-reduce.47
  2017.3 82.4 all-reduce.49
  2167.1 119.3 all-reduce.51
  2291.6 87.2 all-reduce.53
where the time goes:
time: 2410 us; the launch traced here: 2400 us
  waiting for transfers between devices  1760 us (73%)
  other arithmetic  380 us (16%)
  matrix products  120 us (5%)
  local copies, waits for them, and re-layouts  117 us (5%)
    psum x18, waiting for transfers between devices, from_root(): return lax.psum(jnp.where(mine, shard, jnp.zeros_like(shard)), axis)  1720 us
    another operation x42, other arithmetic, factor_rows(): factor = jnp.linalg.cholesky(symmetric_block(pivot))  208 us
    another operation x13, other arithmetic, factor_rows(): lax.linalg.triangular_solve(factor, panel_rows, left_side=False, lower=Tr...  118 us
    dot_general x6, matrix products, on_device(): jnp.einsum('rk,ck->rc', below, across, precision=lax.Precision.HIGHEST)  63.6 us
  transfers between devices with their start and end apart: 19, of which 19 were waited for; matrix products, arithmetic and copies ran while one was open for 1% of the time, Pallas kernels for 0%

commit v1 on v0

--- a/solution.py
+++ b/solution.py
@@ -13,7 +13,7 @@
 
 def from_root(shard, axis, root):
     mine = lax.axis_index(axis) == root
-    return lax.psum(jnp.where(mine, shard, jnp.zeros_like(shard)), axis)
+    return lax.all_gather(jnp.where(mine, shard, jnp.zeros_like(shard)), axis).sum(axis=0)
 
 
 def symmetric_block(pivot_block):

time: 2410 us -> 2550 us (1.058)
  local copies, waits for them, and re-layouts: 117 us -> 285 us
  waiting for transfers between devices: 1760 us -> 1680 us
  other arithmetic: 380 us -> 440 us
    psum x18 -> x0, waiting for transfers between devices: 1720 us -> none  [from_root(): return lax.psum(jnp.where(mine, shard, jnp.zeros_like(shard)), axis)]
    all_gather x0 -> x18, waiting for transfers between devices: none -> 1640 us  [from_root(): lax.all_gather(jnp.where(mine, shard, jnp.zeros_like(shard)), axis)]
    unnamed x47 -> x55, local copies, waits for them, and re-layouts: 24.9 us -> 195 us
    reduce_sum x0 -> x18, other arithmetic: none -> 64.3 us  [from_root(): lax.all_gather(jnp.where(mine, shard, jnp.zeros_like(shard)), axis)]
where the time goes in v1:
time: 2550 us; the launch traced here: 2540 us
  waiting for transfers between devices  1680 us (66%)
  other arithmetic  440 us (17%)
  local copies, waits for them, and re-layouts  285 us (11%)
  matrix products  107 us (4%)
    all_gather x18, waiting for transfers between devices, from_root(): lax.all_gather(jnp.where(mine, shard, jnp.zeros_like(shard)), axis)  1640 us
    another operation x42, other arithmetic, factor_rows(): factor = jnp.linalg.cholesky(symmetric_block(pivot))  208 us
    unnamed x55, local copies, waits for them, and re-layouts  195 us
    another operation x13, other arithmetic, factor_rows(): lax.linalg.triangular_solve(factor, panel_rows, left_side=False, lower=Tr...  118 us
    reduce_sum x18, other arithmetic, from_root(): lax.all_gather(jnp.where(mine, shard, jnp.zeros_like(shard)), axis)  64.3 us
  transfers between devices with their start and end apart: 19, of which 19 were waited for; matrix products, arithmetic and copies ran while one was open for 1% of the time, Pallas kernels for 0%

profile of v1, /device:TPU:0, one launch (start us, length us, event | category | flops | bytes accessed | tf_op | source)
XLA Modules:
  0.0 2537.6 jit_solution(7345890649236793686)
XLA Ops:
  19.3 39.0 %collective-permute-done = f32[4,256,512]{2,1,0:T(8,128)} collective-permute-done((f32[4,256,512]{2,1,0:T(8,128)S(1)}, f32[4,256,512]{2,1,0:T(8,128)}, u32[]{:S(2)}, u32[]{:S(2)}) %collective-permute-start) | collective-permute-done | bytes 2097184 | tf_op jit(solution)/shard_map/ppermute | solution.py:11
  126.4 59.5 %all-gather.43.cloned.1.call-done = f32[2048,256]{0,1:T(8,128)} async-done(((f32[256,256]{0,1:T(8,128)}), f32[2048,256]{0,1:T(8,128)}) %all-gather.43.cloned.1.call-update) | async-done | bytes 2097168 | tf_op jit(solution)/shard_map/all_gather | solution.py:16
  256.1 130.1 %all-gather.45.cloned.1.call-done = f32[24576,256]{0,1:T(8,128)} async-done(((f32[1536,256]{0,1:T(8,128)}), f32[24576,256]{0,1:T(8,128)}) %all-gather.45.cloned.1.call-update) | async-done | bytes 25165840 | tf_op jit(solution)/shard_map/all_gather | solution.py:16
  386.2 26.0 %copy.351 = f32[32,8,16,1536]{3,2,1,0:T(8,128)S(1)} copy(f32[32,8,16,1536]{3,1,2,0:T(8,128)} %bitcast.368) | data formatting | bytes 50331648
  424.8 87.9 %all-gather.31.cloned.1.call-done = f32[8,768,256]{2,1,0:T(8,128)} async-done(((f32[1,768,256]{2,1,0:T(8,128)}), f32[8,768,256]{2,1,0:T(8,128)}) %all-gather.31.cloned.1.call-update) | async-done | bytes 6291472 | tf_op jit(solution)/shard_map/all_gather | solution.py:16
  529.5 55.1 %all-gather.47.cloned.1.call-done = f32[2048,256]{0,1:T(8,128)} async-done(((f32[256,256]{0,1:T(8,128)}), f32[2048,256]{0,1:T(8,128)}) %all-gather.47.cloned.1.call-update) | async-done | bytes 2097168 | tf_op jit(solution)/shard_map/all_gather | solution.py:16
  652.5 130.1 %all-gather.49.cloned.1.call-done = f32[24576,256]{0,1:T(8,128)} async-done(((f32[1536,256]{0,1:T(8,128)}), f32[24576,256]{0,1:T(8,128)}) %all-gather.49.cloned.1.call-update) | async-done | bytes 25165840 | tf_op jit(solution)/shard_map/all_gather | solution.py:16
  782.6 26.0 %copy.353 = f32[32,8,16,1536]{3,2,1,0:T(8,128)S(1)} copy(f32[32,8,16,1536]{3,1,2,0:T(8,128)} %bitcast.369) | data formatting | bytes 50331648
  820.5 88.6 %all-gather.33.cloned.1.call-done = f32[8,768,256]{2,1,0:T(8,128)} async-done(((f32[1,768,256]{2,1,0:T(8,128)}), f32[8,768,256]{2,1,0:T(8,128)}) %all-gather.33.cloned.1.call-update) | async-done | bytes 6291472 | tf_op jit(solution)/shard_map/all_gather | solution.py:16
  925.3 55.1 %all-gather.51.cloned.1.call-done = f32[2048,256]{0,1:T(8,128)} async-done(((f32[256,256]{0,1:T(8,128)}), f32[2048,256]{0,1:T(8,128)}) %all-gather.51.cloned.1.call-update) | async-done | bytes 2097168 | tf_op jit(solution)/shard_map/all_gather | solution.py:16
  1048.2 130.1 %all-gather.53.cloned.1.call-done = f32[24576,256]{0,1:T(8,128)} async-done(((f32[1536,256]{0,1:T(8,128)}), f32[24576,256]{0,1:T(8,128)}) %all-gather.53.cloned.1.call-update) | async-done | bytes 25165840 | tf_op jit(solution)/shard_map/all_gather | solution.py:16
  1178.3 26.0 %copy.355 = f32[32,8,16,1536]{3,2,1,0:T(8,128)S(1)} copy(f32[32,8,16,1536]{3,1,2,0:T(8,128)} %bitcast.370) | data formatting | bytes 50331648
  1221.3 86.0 %all-gather.35.cloned.1.call-done = f32[8,768,256]{2,1,0:T(8,128)} async-done(((f32[1,768,256]{2,1,0:T(8,128)}), f32[8,768,256]{2,1,0:T(8,128)}) %all-gather.35.cloned.1.call-update) | async-done | bytes 6291472 | tf_op jit(solution)/shard_map/all_gather | solution.py:16
  1325.7 55.1 %all-gather.55.cloned.1.call-done = f32[2048,256]{0,1:T(8,128)} async-done(((f32[256,256]{0,1:T(8,128)}), f32[2048,256]{0,1:T(8,128)}) %all-gather.55.cloned.1.call-update) | async-done | bytes 2097168 | tf_op jit(solution)/shard_map/all_gather | solution.py:16
  1448.5 130.1 %all-gather.57.cloned.1.call-done = f32[24576,256]{0,1:T(8,128)} async-done(((f32[1536,256]{0,1:T(8,128)}), f32[24576,256]{0,1:T(8,128)}) %all-gather.57.cloned.1.call-update) | async-done | bytes 25165840 | tf_op jit(solution)/shard_map/all_gather | solution.py:16
  1578.6 26.0 %copy.357 = f32[32,8,16,1536]{3,2,1,0:T(8,128)S(1)} copy(f32[32,8,16,1536]{3,1,2,0:T(8,128)} %bitcast.371) | data formatting | bytes 50331648
  1621.6 86.0 %all-gather.37.cloned.1.call-done = f32[8,768,256]{2,1,0:T(8,128)} async-done(((f32[1,768,256]{2,1,0:T(8,128)}), f32[8,768,256]{2,1,0:T(8,128)}) %all-gather.37.cloned.1.call-update) | async-done | bytes 6291472 | tf_op jit(solution)/shard_map/all_gather | solution.py:16
  1726.0 55.1 %all-gather.59.cloned.1.call-done = f32[2048,256]{0,1:T(8,128)} async-done(((f32[256,256]{0,1:T(8,128)}), f32[2048,256]{0,1:T(8,128)}) %all-gather.59.cloned.1.call-update) | async-done | bytes 2097168 | tf_op jit(solution)/shard_map/all_gather | solution.py:16
  1848.8 130.1 %all-gather.61.cloned.1.call-done = f32[24576,256]{0,1:T(8,128)} async-done(((f32[1536,256]{0,1:T(8,128)}), f32[24576,256]{0,1:T(8,128)}) %all-gather.61.cloned.1.call-update) | async-done | bytes 25165840 | tf_op jit(solution)/shard_map/all_gather | solution.py:16
  1978.9 26.0 %copy.359 = f32[32,8,16,1536]{3,2,1,0:T(8,128)S(1)} copy(f32[32,8,16,1536]{3,1,2,0:T(8,128)} %bitcast.372) | data formatting | bytes 50331648
  2021.9 86.0 %all-gather.39.cloned.1.call-done = f32[8,768,256]{2,1,0:T(8,128)} async-done(((f32[1,768,256]{2,1,0:T(8,128)}), f32[8,768,256]{2,1,0:T(8,128)}) %all-gather.39.cloned.1.call-update) | async-done | bytes 6291472 | tf_op jit(solution)/shard_map/all_gather | solution.py:16
  2126.3 55.1 %all-gather.63.cloned.1.call-done = f32[2048,256]{0,1:T(8,128)} async-done(((f32[256,256]{0,1:T(8,128)}), f32[2048,256]{0,1:T(8,128)}) %all-gather.63.cloned.1.call-update) | async-done | bytes 2097168 | tf_op jit(solution)/shard_map/all_gather | solution.py:16
  2249.2 130.1 %all-gather.65.cloned.1.call-done = f32[24576,256]{0,1:T(8,128)} async-done(((f32[1536,256]{0,1:T(8,128)}), f32[24576,256]{0,1:T(8,128)}) %all-gather.65.cloned.1.call-update) | async-done | bytes 25165840 | tf_op jit(solution)/shard_map/all_gather | solution.py:16
  2422.3 86.1 %all-gather.41.cloned.1.call-done = f32[8,768,256]{2,1,0:T(8,128)} async-done(((f32[1,768,256]{2,1,0:T(8,128)}), f32[8,768,256]{2,1,0:T(8,128)}) %all-gather.41.cloned.1.call-update) | async-done | bytes 6291472 | tf_op jit(solution)/shard_map/all_gather | solution.py:16
  (411 shorter events, 733.7 us)
Async XLA Ops:
  6.5 179.4 %all-gather.43.cloned.1.call-start = ((), (), s32[]{:S(2)}) async-start(), calls=%async_computation.6 | async-start | bytes 2359296 | tf_op jit(solution)/shard_map/all_gather | solution.py:16
  9.2 49.1 %collective-permute-start = (f32[4,256,512]{2,1,0:T(8,128)S(1)}, f32[4,256,512]{2,1,0:T(8,128)}, u32[]{:S(2)}, u32[]{:S(2)}) collective-permute-start(f32[4,256,512]{2,1,0:T(8,128)S(1)} %select_bitcast_fusion), channel_id=1, source_target_pairs={{0,64},{16,80},{32,96},{48,112},{64,0},{80,16},{96,32},{112,48},{1... | collective-permute-start | bytes 6291464 | tf_op jit(solution)/shard_map/ppermute | solution.py:11
  125.9 260.3 %all-gather.45.cloned.1.call-start = ((), (), s32[]{:S(2)}) async-start(), calls=%async_computation.7 | async-start | bytes 26738688 | tf_op jit(solution)/shard_map/all_gather | solution.py:16
  256.0 256.7 %all-gather.31.cloned.1.call-start = ((), (), s32[]{:S(2)}) async-start(), calls=%async_computation | async-start | bytes 7077888 | tf_op jit(solution)/shard_map/all_gather | solution.py:16
  422.0 162.6 %all-gather.47.cloned.1.call-start = ((), (), s32[]{:S(2)}) async-start(), calls=%async_computation.8 | async-start | bytes 2359296 | tf_op jit(solution)/shard_map/all_gather | solution.py:16
  528.3 121.2 %copy-start.5 = (f32[1536,256]{0,1:T(8,128)}, f32[1536,256]{0,1:T(8,128)S(1)}, u32[]{:S(2)}) copy-start(f32[1536,256]{0,1:T(8,128)S(1)} %get-tuple-element.194) | copy-start | bytes 4718596
  529.1 253.5 %all-gather.49.cloned.1.call-start = ((), (), s32[]{:S(2)}) async-start(), calls=%async_computation.9 | async-start | bytes 26738688 | tf_op jit(solution)/shard_map/all_gather | solution.py:16
  652.4 256.6 %all-gather.33.cloned.1.call-start = ((), (), s32[]{:S(2)}) async-start(), calls=%async_computation.1 | async-start | bytes 7077888 | tf_op jit(solution)/shard_map/all_gather | solution.py:16
  818.4 162.0 %all-gather.51.cloned.1.call-start = ((), (), s32[]{:S(2)}) async-start(), calls=%async_computation.10 | async-start | bytes 2359296 | tf_op jit(solution)/shard_map/all_gather | solution.py:16
  924.8 253.5 %all-gather.53.cloned.1.call-start = ((), (), s32[]{:S(2)}) async-start(), calls=%async_computation.11 | async-start | bytes 26738688 | tf_op jit(solution)/shard_map/all_gather | solution.py:16
  1048.2 259.2 %all-gather.35.cloned.1.call-start = ((), (), s32[]{:S(2)}) async-start(), calls=%async_computation.2 | async-start | bytes 7077888 | tf_op jit(solution)/shard_map/all_gather | solution.py:16
  1216.6 164.2 %all-gather.55.cloned.1.call-start = ((), (), s32[]{:S(2)}) async-start(), calls=%async_computation.12 | async-start | bytes 2359296 | tf_op jit(solution)/shard_map/all_gather | solution.py:16
  1325.3 253.3 %all-gather.57.cloned.1.call-start = ((), (), s32[]{:S(2)}) async-start(), calls=%async_computation.13 | async-start | bytes 26738688 | tf_op jit(solution)/shard_map/all_gather | solution.py:16
  1384.2 60.3 %copy-start.2 = (f32[1536,256]{0,1:T(8,128)S(1)}, f32[1536,256]{0,1:T(8,128)}, u32[]{:S(2)}) copy-start(f32[1536,256]{0,1:T(8,128)} %copy-done.1) | copy-start | bytes 4718596
  1448.5 259.2 %all-gather.37.cloned.1.call-start = ((), (), s32[]{:S(2)}) async-start(), calls=%async_computation.3 | async-start | bytes 7077888 | tf_op jit(solution)/shard_map/all_gather | solution.py:16
  1616.9 164.2 %all-gather.59.cloned.1.call-start = ((), (), s32[]{:S(2)}) async-start(), calls=%async_computation.14 | async-start | bytes 2359296 | tf_op jit(solution)/shard_map/all_gather | solution.py:16
  1725.6 253.3 %all-gather.61.cloned.1.call-start = ((), (), s32[]{:S(2)}) async-start(), calls=%async_computation.15 | async-start | bytes 26738688 | tf_op jit(solution)/shard_map/all_gather | solution.py:16
  1784.5 60.3 %copy-start.4 = (f32[1536,256]{0,1:T(8,128)S(1)}, f32[1536,256]{0,1:T(8,128)}, u32[]{:S(2)}) copy-start(f32[1536,256]{0,1:T(8,128)} %copy-done.3) | copy-start | bytes 4718596
  1848.8 259.2 %all-gather.39.cloned.1.call-start = ((), (), s32[]{:S(2)}) async-start(), calls=%async_computation.4 | async-start | bytes 7077888 | tf_op jit(solution)/shard_map/all_gather | solution.py:16
  2017.2 164.2 %all-gather.63.cloned.1.call-start = ((), (), s32[]{:S(2)}) async-start(), calls=%async_computation.16 | async-start | bytes 2359296 | tf_op jit(solution)/shard_map/all_gather | solution.py:16
  2125.9 253.5 %all-gather.65.cloned.1.call-start = ((), (), s32[]{:S(2)}) async-start(), calls=%async_computation.17 | async-start | bytes 26738688 | tf_op jit(solution)/shard_map/all_gather | solution.py:16
  2184.8 60.4 %copy-start.8 = (f32[1536,256]{0,1:T(8,128)S(1)}, f32[1536,256]{0,1:T(8,128)}, u32[]{:S(2)}) copy-start(f32[1536,256]{0,1:T(8,128)} %copy-done.7) | copy-start | bytes 4718596
  2249.2 259.2 %all-gather.41.cloned.1.call-start = ((), (), s32[]{:S(2)}) async-start(), calls=%async_computation.5 | async-start | bytes 7077888 | tf_op jit(solution)/shard_map/all_gather | solution.py:16
  2512.6 8.0 copy-start.15
  (15 other events, 83.4 us)
Sparse Core Ops, SparseCore 0:
  126.0 59.8 all-gather.42
  256.1 129.9 all-gather.44
  422.1 90.5 all-gather.30
  529.2 55.3 all-gather.46
  652.6 129.9 all-gather.48
  818.5 90.5 all-gather.32
  925.0 55.3 all-gather.50
  1048.3 129.9 all-gather.52
  1216.7 90.5 all-gather.34
  1325.4 55.3 all-gather.54
  1448.6 129.9 all-gather.56
  1617.0 90.5 all-gather.36
  1725.7 55.3 all-gather.58
  1848.9 129.9 all-gather.60
  2017.3 90.5 all-gather.38
  2126.0 55.3 all-gather.62
  2249.3 129.9 all-gather.64
  2417.8 90.5 all-gather.40
